TPU v7x, 256 devices: a whole 4x4x8 slice. The times are simulated.
256 devices in a mesh: az: 64 (over x, z, core), rg: 4 (over y).
Axes of the slice: x: 4, y: 4, z: 8, core: 2. Of those that a mesh axis runs over, the one named last changes fastest.
Arguments:
- echoes: bfloat16 [2, 2048, 32768], P(None, 'rg', 'az'), may hold values from -6 to 6
- coef_table: bfloat16 [8, 5, 128, 128], replicated, may hold values from -0.3125 to 0.3125
- kern_id: int32 [256], replicated, may hold values from 0 to 7
- band_lo: int32 [256], replicated, may hold values from -2 to 2, as said below
- band_width: int32 [256], replicated, may hold values from 1 to 5
- rate: float32 [2048], P('rg'), may hold values from 4 to 40
Outputs:
- image: bfloat16 [2, 2048, 32768], P(None, ('rg', 'az'))
Inputs may be any that keep to these rules, and one draw needn't show every extreme that they name: band_lo[b] + band_width[b] - 1 <= 2 for every frequency block b.
All inputs are finite; a program needn't handle non-finite values.
Results may differ from a plain program's by a relative error of at most 0.0095.
Values may be sent and summed in bfloat16 or wider, within the bound.
No kernel may reach another device: no remote copies, remote signals or barrier semaphores. Data moves between devices by JAX's collectives and lax.ppermute only.
A program may use at most 64 MiB of HBM per device.

v0:
```python
import math
import jax
import jax.numpy as jnp
from jax import lax
from jax.sharding import PartitionSpec as P

A = 32768
P_SIZE = 512
Q = 64
TILE = 128
FB = 128
FBLK = 256
HT = 2
WMAX = 5
TWO_PI = 2.0 * math.pi


def padded_2(block, sides, width):
    for axis, dim in sides:
        count = lax.axis_size(axis)
        forward = [(i, i + 1) for i in range(count - 1)]
        backward = [(target, source) for source, target in forward]
        low = lax.ppermute(
            lax.slice_in_dim(block, block.shape[dim] - width, None, axis=dim), axis, forward
        )
        high = lax.ppermute(lax.slice_in_dim(block, 0, width, axis=dim), axis, backward)
        block = jnp.concatenate([low, block, high], axis=dim)
    return block


def rotation(first, second, length):
    product = lax.broadcasted_iota(jnp.int32, (first, second), 0) * lax.broadcasted_iota(
        jnp.int32, (first, second), 1
    )
    angle = (product % length).astype(jnp.float32) * (TWO_PI / length)
    return (jnp.cos(angle), jnp.sin(angle))


def tables():
    cosine_first, sine_first = rotation(P_SIZE, P_SIZE, P_SIZE)
    cosine_second, sine_second = rotation(Q, Q, Q)
    cosine_twist, sine_twist = rotation(Q, P_SIZE, A)
    scale_first = 1.0 / math.sqrt(P_SIZE)
    scale_second = 1.0 / math.sqrt(Q)
    return (
        (cosine_first * scale_first).astype(jnp.bfloat16),
        (sine_first * scale_first).astype(jnp.bfloat16),
        (cosine_second * scale_second).astype(jnp.bfloat16),
        (sine_second * scale_second).astype(jnp.bfloat16),
        cosine_twist,
        sine_twist,
    )


def contract(form, left, right):
    return jnp.einsum(form, left, right, preferred_element_type=jnp.float32)


def forward(planes, factors):
    cosine_first, sine_first, cosine_second, sine_second, cosine_twist, sine_twist = factors
    width = planes.shape[1]
    grid = planes.reshape(2, width, P_SIZE, Q)
    real_part = grid[0]
    imaginary = grid[1]
    first_real = contract("cpq,pf->cqf", real_part, cosine_first) + contract(
        "cpq,pf->cqf", imaginary, sine_first
    )
    first_imaginary = contract("cpq,pf->cqf", imaginary, cosine_first) - contract(
        "cpq,pf->cqf", real_part, sine_first
    )
    turned_real = (first_real * cosine_twist + first_imaginary * sine_twist).astype(jnp.bfloat16)
    turned_imaginary = (first_imaginary * cosine_twist - first_real * sine_twist).astype(
        jnp.bfloat16
    )
    second_real = contract("gq,cqf->cgf", cosine_second, turned_real) + contract(
        "gq,cqf->cgf", sine_second, turned_imaginary
    )
    second_imaginary = contract("gq,cqf->cgf", cosine_second, turned_imaginary) - contract(
        "gq,cqf->cgf", sine_second, turned_real
    )
    return jnp.stack([second_real, second_imaginary]).reshape(2, width, A).astype(jnp.bfloat16)


def inverse(planes, factors):
    cosine_first, sine_first, cosine_second, sine_second, cosine_twist, sine_twist = factors
    width = planes.shape[1]
    grid = planes.reshape(2, width, Q, P_SIZE)
    real_part = grid[0]
    imaginary = grid[1]
    first_real = contract("qg,cgf->cqf", cosine_second, real_part) - contract(
        "qg,cgf->cqf", sine_second, imaginary
    )
    first_imaginary = contract("qg,cgf->cqf", cosine_second, imaginary) + contract(
        "qg,cgf->cqf", sine_second, real_part
    )
    turned_real = (first_real * cosine_twist - first_imaginary * sine_twist).astype(jnp.bfloat16)
    turned_imaginary = (first_imaginary * cosine_twist + first_real * sine_twist).astype(
        jnp.bfloat16
    )
    second_real = contract("cqf,fp->cpq", turned_real, cosine_first) - contract(
        "cqf,fp->cpq", turned_imaginary, sine_first
    )
    second_imaginary = contract("cqf,fp->cpq", turned_imaginary, cosine_first) + contract(
        "cqf,fp->cpq", turned_real, sine_first
    )
    return jnp.stack([second_real, second_imaginary]).reshape(2, width, A).astype(jnp.bfloat16)


def body(echoes, coef_table, kern_id, band_lo, band_width, rate):
    factors = tables()
    members = lax.axis_size("az")
    here = lax.axis_index("az")
    range_rows = echoes.shape[1]
    lines = echoes.shape[2]
    columns = range_rows // members
    per_device = FBLK // members
    freq_dev = per_device * FB
    tiles = range_rows // TILE
    grouped = echoes.reshape(2, members, columns, lines)
    piece = lax.all_to_all(grouped, "az", split_axis=1, concat_axis=3, tiled=True)
    spectrum = forward(piece.reshape(2, piece.shape[2], A), factors)
    parted = spectrum.reshape(2, columns, members, freq_dev)
    turned = lax.all_to_all(parted, "az", split_axis=2, concat_axis=1, tiled=True)
    block_first = here * per_device
    block_stride = 1
    local = turned.reshape(2, range_rows, freq_dev)
    rim = HT * TILE
    padded = padded_2(local, (("rg", 1),), rim)

    def one_block(index, result):
        block = block_first + index * block_stride
        lower = band_lo[block]
        width = band_width[block]
        kernel = coef_table[kern_id[block]]
        columns_in = lax.dynamic_slice_in_dim(padded, index * FB, FB, 2)
        empty = jnp.zeros((2, tiles, TILE, FB), jnp.float32)
        total = empty
        for offset in range(WMAX):
            masked = jnp.where(offset < width, kernel[offset], jnp.zeros_like(kernel[offset]))
            start = (HT + lower + offset) * TILE
            slab = lax.dynamic_slice_in_dim(columns_in, start, range_rows, 1).reshape(
                2, tiles, TILE, FB
            )
            total = total + contract("ij,ptjf->ptif", masked, slab)
        moved = total.reshape(2, range_rows, FB)
        signed = (block * FB + lax.broadcasted_iota(jnp.int32, (FB,), 0) + A // 2) % A - A // 2
        doppler = signed.astype(jnp.float32) / A
        phase = rate[:, None] * (doppler * doppler)[None, :] * TWO_PI
        cosine = jnp.cos(phase)
        sine = jnp.sin(phase)
        focused_real = moved[0] * cosine + moved[1] * sine
        focused_imaginary = moved[1] * cosine - moved[0] * sine
        focused = jnp.stack([focused_real, focused_imaginary]).astype(jnp.bfloat16)
        return lax.dynamic_update_slice_in_dim(result, focused, index * FB, 2)

    filtered = lax.fori_loop(
        0, per_device, one_block, jnp.zeros((2, range_rows, freq_dev), jnp.bfloat16)
    )
    returned = filtered.reshape(2, members, columns, 1, freq_dev)
    piece = lax.all_to_all(returned, "az", split_axis=1, concat_axis=3, tiled=True)
    return inverse(piece.reshape(2, piece.shape[2], A), factors)


def solution(mesh):
    in_specs = (P(None, "rg", "az"), P(), P(), P(), P(), P("rg"))
    out_specs = P(None, ("rg", "az"), None)
    return jax.shard_map(body, mesh=mesh, in_specs=in_specs, out_specs=out_specs, check_vma=False)
```

profile of v0, /device:TPU:1, one launch (start us, length us, event | category | flops | bytes accessed | tf_op | source)
XLA Modules:
  0.0 264.5 jit_solution(644591594044299887)
XLA Ops:
  0.0 2.3 copy.28
  2.3 13.0 %all-to-all-start = ((bf16[2,64,8,512]{3,2,0,1:T(8,128)(2,1)}), bf16[2,64,8,512]{3,2,0,1:T(8,128)(2,1)S(1)}, u32[]{:S(2)}, u32[]{:S(2)}) async-start(bf16[2,64,8,512]{3,2,0,1:T(8,128)(2,1)} %copy.28), calls=%async_computation | async-start | bytes 2097152 | tf_op jit(solution)/shard_map/all_to_all | solution.py:120
  15.9 28.0 %all-to-all-done = bf16[2,64,8,512]{3,2,0,1:T(8,128)(2,1)S(1)} async-done(((bf16[2,64,8,512]{3,2,0,1:T(8,128)(2,1)}), bf16[2,64,8,512]{3,2,0,1:T(8,128)(2,1)S(1)}, u32[]{:S(2)}, u32[]{:S(2)}) %all-to-all-start) | async-done | bytes 1048608 | tf_op jit(solution)/shard_map/all_to_all | solution.py:120
  45.0 4.9 %fusion.71 = f32[512,512]{0,1:S(1)} fusion(bf16[512,512]{0,1:T(8,128)(2,1)S(1)} %bitcast.267), kind=kOutput, calls=%fused_computation.113 | convolution fusion | flops 272629760 | bytes 1572864
  49.9 5.7 %fusion.70 = f32[512,512]{0,1} fusion(bf16[512,512]{0,1:T(8,128)(2,1)S(1)} %bitcast.268), kind=kOutput, calls=%fused_computation.112 | convolution fusion | flops 272629760 | bytes 1572864
  56.6 4.9 %fusion.69 = f32[512,512]{0,1:S(1)} fusion(bf16[512,512]{0,1:T(8,128)(2,1)S(1)} %bitcast.269), kind=kOutput, calls=%fused_computation.111 | convolution fusion | flops 272629760 | bytes 1572864
  61.5 5.1 %fusion.72 = f32[512,512]{0,1:S(1)} fusion(bf16[512,512]{0,1:T(8,128)(2,1)S(1)} %bitcast.270), kind=kOutput, calls=%fused_computation.114 | convolution fusion | flops 272629760 | bytes 1572864
  66.6 0.6 fusion.57
  69.5 34.5 %all_to_all.45 = bf16[2,8,64,512]{3,1,0,2:T(8,128)(2,1)S(1)} all-to-all(bf16[2,8,64,512]{3,1,0,2:T(8,128)(2,1)S(1)} %copy.35), channel_id=1, replica_groups=mesh['az'=64,'rg'=4] {'az'}, dimensions={2} | all-to-all | bytes 2097152 | tf_op jit(solution)/shard_map/all_to_all | solution.py:123
  104.2 3.2 %collective-permute-start = (bf16[2,256,512]{2,1,0:T(8,128)(2,1)S(1)}, bf16[2,256,512]{2,1,0:T(8,128)(2,1)S(1)}, u32[]{:S(2)}, u32[]{:S(2)}) collective-permute-start(bf16[2,256,512]{2,1,0:T(8,128)(2,1)S(1)} %get-tuple-element.310), channel_id=1, source_target_pairs={{0,1},{1,2},{2,3},{4,5},{5,6},{6,7},{8,9},{9,10},{10,11},{12,13},{... | collective-permute-start | bytes 1572872 | tf_op jit(solution)/shard_map/ppermute | solution.py:23
  107.5 1.3 collective-permute-start.1
  108.8 9.9 %collective-permute-done = bf16[2,256,512]{2,1,0:T(8,128)(2,1)S(1)} collective-permute-done((bf16[2,256,512]{2,1,0:T(8,128)(2,1)S(1)}, bf16[2,256,512]{2,1,0:T(8,128)(2,1)S(1)}, u32[]{:S(2)}, u32[]{:S(2)}) %collective-permute-start) | collective-permute-done | bytes 524320 | tf_op jit(solution)/shard_map/ppermute | solution.py:23
  118.7 0.8 copy-done.3
  119.5 3.1 %collective-permute-done.1 = bf16[2,256,512]{2,1,0:T(8,128)(2,1)} collective-permute-done((bf16[2,256,512]{2,1,0:T(8,128)(2,1)S(1)}, bf16[2,256,512]{2,1,0:T(8,128)(2,1)}, u32[]{:S(2)}, u32[]{:S(2)}) %collective-permute-start.1) | collective-permute-done | bytes 524320 | tf_op jit(solution)/shard_map/ppermute | solution.py:26
  122.6 1.3 pad_maximum_fusion
  124.0 1.0 broadcast_in_dim.6
  125.0 75.2 %while.16 = (s32[]{:T(128)}, bf16[2,512,512]{2,1,0:T(8,128)(2,1)}, s32[]{:T(128)}, s32[256]{0:T(256)S(1)}, bf16[2,1024,512]{2,1,0:T(8,128)(2,1)S(1)}, /*index=5*...) while((s32[]{:T(128)}, bf16[2,512,512]{2,1,0:T(8,128)(2,1)}, ...), condition=%wide.region_1.2_spmd, body=%wide.region_0.1_spmd.sunk | while | flops 169560240 | bytes 11180494 | solution.py:156
  125.1 0.6 dynamic_slice.117
  128.5 2.0 constant_dynamic-slice_fusion.6
  132.8 0.6 dynamic_slice.119
  133.9 1.0 fusion.226
  135.5 1.2 convolution_add_fusion.10
  137.3 1.2 convolution_add_fusion.11
  139.0 1.2 convolution_add_fusion.12
  140.8 1.0 fusion.227
  141.9 1.3 fusion.230
  143.1 0.7 maximum_dynamic-update-slice_fusion.2
  143.9 0.6 dynamic_slice.117
  147.3 2.0 constant_dynamic-slice_fusion.6
  152.7 1.0 fusion.226
  154.3 1.2 convolution_add_fusion.10
  156.1 1.2 convolution_add_fusion.11
  157.8 1.2 convolution_add_fusion.12
  159.6 1.0 fusion.227
  160.7 1.3 fusion.230
  161.9 0.7 maximum_dynamic-update-slice_fusion.2
  162.7 0.6 dynamic_slice.117
  166.1 2.0 constant_dynamic-slice_fusion.6
  170.4 0.6 dynamic_slice.119
  171.5 1.0 fusion.226
  173.1 1.2 convolution_add_fusion.10
  174.9 1.2 convolution_add_fusion.11
  176.6 1.2 convolution_add_fusion.12
  178.4 1.0 fusion.227
  179.5 1.3 fusion.230
  180.7 0.7 maximum_dynamic-update-slice_fusion.2
  181.5 0.6 dynamic_slice.117
  184.9 2.0 constant_dynamic-slice_fusion.6
  190.3 1.0 fusion.226
  191.9 1.2 convolution_add_fusion.10
  193.7 1.2 convolution_add_fusion.11
  195.4 1.2 convolution_add_fusion.12
  197.2 1.0 fusion.227
  198.3 1.3 fusion.230
  199.5 0.7 maximum_dynamic-update-slice_fusion.2
  200.2 1.4 copy.37
  201.6 35.1 %all_to_all.46 = bf16[2,64,8,1,512]{4,2,0,3,1:T(8,128)(2,1)S(1)} all-to-all(bf16[2,64,8,1,512]{4,2,0,3,1:T(8,128)(2,1)S(1)} %copy.37), channel_id=1, replica_groups=mesh['az'=64,'rg'=4] {'az'}, dimensions={1} | all-to-all | bytes 2097152 | tf_op jit(solution)/shard_map/all_to_all | solution.py:160
  239.2 4.9 %fusion.67 = f32[512,8,64]{0,2,1:T(8,128)S(1)} fusion(bf16[8,64,512]{2,1,0:T(8,128)(2,1)S(1)} %get-tuple-element.308), kind=kOutput, calls=%fused_computation.109 | convolution fusion | flops 272629760 | bytes 1572864 | tf_op jit(solution)/shard_map/cqf,fp->cpq/dot_general | solution.py:56
  244.1 5.7 %fusion.65 = f32[512,8,64]{0,2,1:T(8,128)} fusion(bf16[8,64,512]{2,1,0:T(8,128)(2,1)S(1)} %get-tuple-element.309), kind=kOutput, calls=%fused_computation.107 | convolution fusion | flops 272629760 | bytes 1572864 | tf_op jit(solution)/shard_map/cqf,fp->cpq/dot_general | solution.py:56
  249.8 5.0 %fusion.50 = bf16[8,512,64]{1,2,0:T(8,128)(2,1)S(1)} fusion(f32[512,8,64]{0,2,1:T(8,128)S(1)} %fusion.67, bf16[8,64,512]{2,1,0:T(8,128)(2,1)S(1)} %get-tuple-element.309), kind=kOutput, calls=%fused_computation.78 | convolution fusion | flops 273154048 | bytes 2097152 | tf_op jit(solution)/shard_map/cqf,fp->cpq/dot_general | solution.py:56
  255.3 0.8 stack.39
  256.1 6.0 %fusion.49 = bf16[8,512,64]{1,2,0:T(8,128)(2,1)S(1)} fusion(f32[512,8,64]{0,2,1:T(8,128)} %fusion.65, bf16[8,64,512]{2,1,0:T(8,128)(2,1)S(1)} %get-tuple-element.308), kind=kOutput, calls=%fused_computation.77 | convolution fusion | flops 273154048 | bytes 2097152 | tf_op jit(solution)/shard_map/cqf,fp->cpq/dot_general | solution.py:56
  262.6 0.8 stack.40
  263.4 1.1 pad_maximum_fusion.2
  (52 shorter events, 12.1 us)
Async XLA Ops:
  2.3 41.5 %all-to-all-start = ((bf16[2,64,8,512]{3,2,0,1:T(8,128)(2,1)}), bf16[2,64,8,512]{3,2,0,1:T(8,128)(2,1)S(1)}, u32[]{:S(2)}, u32[]{:S(2)}) async-start(bf16[2,64,8,512]{3,2,0,1:T(8,128)(2,1)} %copy.28), calls=%async_computation | async-start | bytes 2097152 | tf_op jit(solution)/shard_map/all_to_all | solution.py:120
  15.9 50.7 %copy-start = (f32[64,512]{1,0:T(8,128)}, f32[64,512]{1,0:T(8,128)S(1)}, u32[]{:S(2)}) copy-start(f32[64,512]{1,0:T(8,128)S(1)} %get-tuple-element.315) | copy-start | bytes 393220
  61.5 5.1 %copy-start.2 = (f32[512,512]{0,1:S(1)}, f32[512,512]{0,1}, u32[]{:S(2)}) copy-start(f32[512,512]{0,1} %fusion.70) | copy-start | bytes 3145732
  104.2 14.5 %collective-permute-start = (bf16[2,256,512]{2,1,0:T(8,128)(2,1)S(1)}, bf16[2,256,512]{2,1,0:T(8,128)(2,1)S(1)}, u32[]{:S(2)}, u32[]{:S(2)}) collective-permute-start(bf16[2,256,512]{2,1,0:T(8,128)(2,1)S(1)} %get-tuple-element.310), channel_id=1, source_target_pairs={{0,1},{1,2},{2,3},{4,5},{5,6},{6,7},{8,9},{9,10},{10,11},{12,13},{... | collective-permute-start | bytes 1572872 | tf_op jit(solution)/shard_map/ppermute | solution.py:23
  107.5 15.2 %collective-permute-start.1 = (bf16[2,256,512]{2,1,0:T(8,128)(2,1)S(1)}, bf16[2,256,512]{2,1,0:T(8,128)(2,1)}, u32[]{:S(2)}, u32[]{:S(2)}) collective-permute-start(bf16[2,256,512]{2,1,0:T(8,128)(2,1)S(1)} %get-tuple-element.311), channel_id=1, source_target_pairs={{1,0},{2,1},{3,2},{5,4},{6,5},{7,6},{9,8},{10,9},{11,10},{13,12},{... | collective-permute-start | bytes 1572872 | tf_op jit(solution)/shard_map/ppermute | solution.py:26
  108.8 16.2 %copy-start.4 = (f32[512]{0:T(512)S(1)}, f32[512]{0:T(512)}, u32[]{:S(2)}) copy-start(f32[512]{0:T(512)} %param.13) | copy-start | bytes 6148
  108.8 16.2 %copy-start.5 = (s32[256]{0:T(256)S(1)}, s32[256]{0:T(256)}, u32[]{:S(2)}) copy-start(s32[256]{0:T(256)} %param.11) | copy-start | bytes 3076
  108.8 16.2 %copy-start.6 = (s32[256]{0:T(256)S(1)}, s32[256]{0:T(256)}, u32[]{:S(2)}) copy-start(s32[256]{0:T(256)} %param.12) | copy-start | bytes 3076
  108.8 16.2 %copy-start.7 = (s32[256]{0:T(256)S(1)}, s32[256]{0:T(256)}, u32[]{:S(2)}) copy-start(s32[256]{0:T(256)} %param.10) | copy-start | bytes 3076
  118.7 0.8 copy-start.3
  237.7 0.9 copy-start.1
where the time goes:
time: 266 us; the launch traced here: 264 us
  blocking collectives  69.7 us (26%)
  matrix products  67.5 us (25%)
  waiting for transfers between devices  41 us (15%)
  loops' own time  29.9 us (11%)
  local copies, waits for them, and re-layouts  26.9 us (10%)
  starting transfers between devices  17.5 us (7%)
  other arithmetic  11.6 us (4%)
    dot_general x32, matrix products, contract(): return jnp.einsum(form, left, right, preferred_element_type=jnp.float32)  47 us
    all_to_all x1, blocking collectives, body(): lax.all_to_all(returned, 'az', split_axis=1, concat_axis=3, tiled=True)  35.1 us
    all_to_all x1, blocking collectives, body(): lax.all_to_all(parted, 'az', split_axis=2, concat_axis=1, tiled=True)  34.5 us
    another operation x1, loops' own time, body(): lax.fori_loop(0, per_device, one_block, jnp.zeros((2, range_rows, freq_de...  29.9 us
    all_to_all x1, waiting for transfers between devices, body(): lax.all_to_all(grouped, 'az', split_axis=1, concat_axis=3, tiled=True)  28 us
    unnamed x4, matrix products  20.5 us
    all_to_all x1, starting transfers between devices, body(): lax.all_to_all(grouped, 'az', split_axis=1, concat_axis=3, tiled=True)  13 us
    ppermute x1, waiting for transfers between devices, padded_2(): lax.ppermute(lax.slice_in_dim(block, block.shape[dim] - width, None, axis...  9.87 us
  transfers between devices with their start and end apart: 3, of which 3 were waited for; matrix products, arithmetic and copies ran while one was open for 0% of the time, Pallas kernels for 0%

commit v1 on v0

--- a/solution.py
+++ b/solution.py
@@ -120,7 +120,10 @@
     piece = lax.all_to_all(grouped, "az", split_axis=1, concat_axis=3, tiled=True)
     spectrum = forward(piece.reshape(2, piece.shape[2], A), factors)
     parted = spectrum.reshape(2, columns, members, freq_dev)
-    turned = lax.all_to_all(parted, "az", split_axis=2, concat_axis=1, tiled=True)
+    turned = jnp.concatenate(
+        lax.all_to_all(jnp.stack(jnp.split(parted, lax.axis_size("az"), axis=2)), "az", 0, 0),
+        axis=1,
+    )
     block_first = here * per_device
     block_stride = 1
     local = turned.reshape(2, range_rows, freq_dev)

time: 266 us -> 275 us (1.034)
  loops' own time: 29.9 us -> 34.3 us
    another operation x1, loops' own time: 29.9 us -> 34.3 us  [body(): lax.fori_loop(0, per_device, one_block, jnp.zeros((2, range_rows, freq_de...]
where the time goes in v1:
time: 275 us; the launch traced here: 273 us
  blocking collectives  69.7 us (25%)
  matrix products  67.5 us (25%)
  waiting for transfers between devices  41 us (15%)
  loops' own time  34.3 us (12%)
  local copies, waits for them, and re-layouts  27.8 us (10%)
  starting transfers between devices  17.5 us (6%)
  other arithmetic  14.3 us (5%)
    dot_general x32, matrix products, contract(): return jnp.einsum(form, left, right, preferred_element_type=jnp.float32)  47 us
    all_to_all x1, blocking collectives, body(): lax.all_to_all(returned, 'az', split_axis=1, concat_axis=3, tiled=True)  35.2 us
    all_to_all x1, blocking collectives, body(): lax.all_to_all(jnp.stack(jnp.split(parted, lax.axis_size('az'), axis=2)),...  34.5 us
    another operation x1, loops' own time, body(): lax.fori_loop(0, per_device, one_block, jnp.zeros((2, range_rows, freq_de...  34.3 us
    all_to_all x1, waiting for transfers between devices, body(): lax.all_to_all(grouped, 'az', split_axis=1, concat_axis=3, tiled=True)  28 us
    unnamed x4, matrix products  20.5 us
    all_to_all x1, starting transfers between devices, body(): lax.all_to_all(grouped, 'az', split_axis=1, concat_axis=3, tiled=True)  13 us
    ppermute x1, waiting for transfers between devices, padded_2(): lax.ppermute(lax.slice_in_dim(block, block.shape[dim] - width, None, axis...  9.87 us
  transfers between devices with their start and end apart: 3, of which 3 were waited for; matrix products, arithmetic and copies ran while one was open for 0% of the time, Pallas kernels for 0%

profile of v1, /device:TPU:1, one launch (start us, length us, event | category | flops | bytes accessed | tf_op | source)
XLA Modules:
  0.0 273.0 jit_solution(8737664255932335197)
XLA Ops:
  0.0 2.3 copy.1774
  2.3 13.0 %all-to-all-start = ((bf16[2,64,8,512]{3,2,0,1:T(8,128)(2,1)}), bf16[2,64,8,512]{3,2,0,1:T(8,128)(2,1)S(1)}, u32[]{:S(2)}, u32[]{:S(2)}) async-start(bf16[2,64,8,512]{3,2,0,1:T(8,128)(2,1)} %copy.1774), calls=%async_computation | async-start | bytes 2097152 | tf_op jit(solution)/shard_map/all_to_all | solution.py:120
  15.9 28.0 %all-to-all-done = bf16[2,64,8,512]{3,2,0,1:T(8,128)(2,1)S(1)} async-done(((bf16[2,64,8,512]{3,2,0,1:T(8,128)(2,1)}), bf16[2,64,8,512]{3,2,0,1:T(8,128)(2,1)S(1)}, u32[]{:S(2)}, u32[]{:S(2)}) %all-to-all-start) | async-done | bytes 1048608 | tf_op jit(solution)/shard_map/all_to_all | solution.py:120
  45.5 4.9 %fusion.71 = f32[512,512]{0,1:S(1)} fusion(bf16[512,512]{0,1:T(8,128)(2,1)S(1)} %bitcast.393), kind=kOutput, calls=%fused_computation.239 | convolution fusion | flops 272629760 | bytes 1572864
  50.4 5.7 %fusion.70 = f32[512,512]{0,1} fusion(bf16[512,512]{0,1:T(8,128)(2,1)S(1)} %bitcast.394), kind=kOutput, calls=%fused_computation.238 | convolution fusion | flops 272629760 | bytes 1572864
  56.9 4.9 %fusion.69 = f32[512,512]{0,1:S(1)} fusion(bf16[512,512]{0,1:T(8,128)(2,1)S(1)} %bitcast.395), kind=kOutput, calls=%fused_computation.237 | convolution fusion | flops 272629760 | bytes 1572864
  61.8 5.1 %fusion.72 = f32[512,512]{0,1:S(1)} fusion(bf16[512,512]{0,1:T(8,128)(2,1)S(1)} %bitcast.396), kind=kOutput, calls=%fused_computation.240 | convolution fusion | flops 272629760 | bytes 1572864
  72.8 34.5 %all_to_all.35 = bf16[64,2,8,1,512]{4,2,1,3,0:T(8,128)(2,1)S(1)} all-to-all(bf16[64,2,8,1,512]{4,2,1,3,0:T(8,128)(2,1)S(1)} %constant_dynamic-update-slice_fusion), channel_id=1, replica_groups=mesh['az'=64,'rg'=4] {'az'}, dimensions={0} | all-to-all | bytes 2097152 | tf_op jit(solution)/shard_map/all_to_all | solution.py:124
  107.5 3.2 %collective-permute-start = (bf16[2,256,512]{2,1,0:T(8,128)(2,1)S(1)}, bf16[2,256,512]{2,1,0:T(8,128)(2,1)S(1)}, u32[]{:S(2)}, u32[]{:S(2)}) collective-permute-start(bf16[2,256,512]{2,1,0:T(8,128)(2,1)S(1)} %get-tuple-element.310), channel_id=1, source_target_pairs={{0,1},{1,2},{2,3},{4,5},{5,6},{6,7},{8,9},{9,10},{10,11},{12,13},{... | collective-permute-start | bytes 1572872 | tf_op jit(solution)/shard_map/ppermute | solution.py:23
  110.8 1.3 collective-permute-start.1
  112.1 9.9 %collective-permute-done = bf16[2,256,512]{2,1,0:T(8,128)(2,1)S(1)} collective-permute-done((bf16[2,256,512]{2,1,0:T(8,128)(2,1)S(1)}, bf16[2,256,512]{2,1,0:T(8,128)(2,1)S(1)}, u32[]{:S(2)}, u32[]{:S(2)}) %collective-permute-start) | collective-permute-done | bytes 524320 | tf_op jit(solution)/shard_map/ppermute | solution.py:23
  122.0 0.8 copy-done.3
  122.8 3.1 %collective-permute-done.1 = bf16[2,256,512]{2,1,0:T(8,128)(2,1)} collective-permute-done((bf16[2,256,512]{2,1,0:T(8,128)(2,1)S(1)}, bf16[2,256,512]{2,1,0:T(8,128)(2,1)}, u32[]{:S(2)}, u32[]{:S(2)}) %collective-permute-start.1) | collective-permute-done | bytes 524320 | tf_op jit(solution)/shard_map/ppermute | solution.py:26
  125.9 1.3 pad_maximum_fusion
  127.3 1.0 broadcast_in_dim.6
  128.3 80.4 %while.16 = (s32[]{:T(128)}, bf16[2,512,512]{2,1,0:T(8,128)(2,1)}, s32[]{:T(128)}, s32[256]{0:T(256)S(1)}, bf16[2,1024,512]{2,1,0:T(8,128)(2,1)S(1)}, /*index=5*...) while((s32[]{:T(128)}, bf16[2,512,512]{2,1,0:T(8,128)(2,1)}, ...), condition=%wide.region_1.2_spmd, body=%wide.region_0.1_spmd.sunk | while | flops 169560240 | bytes 11180494 | solution.py:159
  128.4 0.7 dynamic_slice.117
  132.4 2.0 constant_dynamic-slice_fusion.6
  134.4 0.6 dynamic_slice.118
  137.0 0.7 dynamic_slice.119
  138.3 1.0 fusion.290
  139.9 1.2 convolution_add_fusion.10
  141.7 1.2 convolution_add_fusion.11
  143.6 1.2 convolution_add_fusion.12
  145.4 1.0 fusion.291
  146.5 1.3 fusion.294
  147.7 0.7 maximum_dynamic-update-slice_fusion.2
  152.5 2.0 constant_dynamic-slice_fusion.6
  157.1 0.7 dynamic_slice.119
  158.4 1.0 fusion.290
  160.0 1.2 convolution_add_fusion.10
  161.8 1.2 convolution_add_fusion.11
  163.7 1.2 convolution_add_fusion.12
  165.5 1.0 fusion.291
  166.6 1.3 fusion.294
  167.8 0.7 maximum_dynamic-update-slice_fusion.2
  172.6 2.0 constant_dynamic-slice_fusion.6
  177.2 0.7 dynamic_slice.119
  178.5 1.0 fusion.290
  180.1 1.2 convolution_add_fusion.10
  181.9 1.2 convolution_add_fusion.11
  183.8 1.2 convolution_add_fusion.12
  185.6 1.0 fusion.291
  186.7 1.3 fusion.294
  187.9 0.7 maximum_dynamic-update-slice_fusion.2
  192.7 2.0 constant_dynamic-slice_fusion.6
  194.7 0.6 dynamic_slice.118
  197.3 0.7 dynamic_slice.119
  198.6 1.0 fusion.290
  200.2 1.2 convolution_add_fusion.10
  202.0 1.2 convolution_add_fusion.11
  203.9 1.2 convolution_add_fusion.12
  205.7 1.0 fusion.291
  206.8 1.3 fusion.294
  208.0 0.7 maximum_dynamic-update-slice_fusion.2
  208.8 1.4 copy.1781
  210.1 35.2 %all_to_all.36 = bf16[2,64,8,1,512]{4,2,0,3,1:T(8,128)(2,1)S(1)} all-to-all(bf16[2,64,8,1,512]{4,2,0,3,1:T(8,128)(2,1)S(1)} %copy.1781), channel_id=1, replica_groups=mesh['az'=64,'rg'=4] {'az'}, dimensions={1} | all-to-all | bytes 2097152 | tf_op jit(solution)/shard_map/all_to_all | solution.py:163
  247.7 4.9 %fusion.67 = f32[512,8,64]{0,2,1:T(8,128)S(1)} fusion(bf16[8,64,512]{2,1,0:T(8,128)(2,1)S(1)} %get-tuple-element.308), kind=kOutput, calls=%fused_computation.235 | convolution fusion | flops 272629760 | bytes 1572864 | tf_op jit(solution)/shard_map/cqf,fp->cpq/dot_general | solution.py:56
  252.6 5.7 %fusion.65 = f32[512,8,64]{0,2,1:T(8,128)} fusion(bf16[8,64,512]{2,1,0:T(8,128)(2,1)S(1)} %get-tuple-element.309), kind=kOutput, calls=%fused_computation.233 | convolution fusion | flops 272629760 | bytes 1572864 | tf_op jit(solution)/shard_map/cqf,fp->cpq/dot_general | solution.py:56
  258.3 5.0 %fusion.50 = bf16[8,512,64]{1,2,0:T(8,128)(2,1)S(1)} fusion(f32[512,8,64]{0,2,1:T(8,128)S(1)} %fusion.67, bf16[8,64,512]{2,1,0:T(8,128)(2,1)S(1)} %get-tuple-element.309), kind=kOutput, calls=%fused_computation.204 | convolution fusion | flops 273154048 | bytes 2097152 | tf_op jit(solution)/shard_map/cqf,fp->cpq/dot_general | solution.py:56
  263.8 0.8 stack.299
  264.6 6.0 %fusion.49 = bf16[8,512,64]{1,2,0:T(8,128)(2,1)S(1)} fusion(f32[512,8,64]{0,2,1:T(8,128)} %fusion.65, bf16[8,64,512]{2,1,0:T(8,128)(2,1)S(1)} %get-tuple-element.308), kind=kOutput, calls=%fused_computation.203 | convolution fusion | flops 273154048 | bytes 2097152 | tf_op jit(solution)/shard_map/cqf,fp->cpq/dot_general | solution.py:56
  271.1 0.8 stack.300
  271.9 1.1 pad_maximum_fusion.1
  (121 shorter events, 15.3 us)
Async XLA Ops:
  2.3 41.5 %all-to-all-start = ((bf16[2,64,8,512]{3,2,0,1:T(8,128)(2,1)}), bf16[2,64,8,512]{3,2,0,1:T(8,128)(2,1)S(1)}, u32[]{:S(2)}, u32[]{:S(2)}) async-start(bf16[2,64,8,512]{3,2,0,1:T(8,128)(2,1)} %copy.1774), calls=%async_computation | async-start | bytes 2097152 | tf_op jit(solution)/shard_map/all_to_all | solution.py:120
  15.9 51.0 %copy-start = (f32[64,512]{1,0:T(8,128)}, f32[64,512]{1,0:T(8,128)S(1)}, u32[]{:S(2)}) copy-start(f32[64,512]{1,0:T(8,128)S(1)} %get-tuple-element.378) | copy-start | bytes 393220
  61.8 5.1 %copy-start.2 = (f32[512,512]{0,1:S(1)}, f32[512,512]{0,1}, u32[]{:S(2)}) copy-start(f32[512,512]{0,1} %fusion.70) | copy-start | bytes 3145732
  107.5 14.5 %collective-permute-start = (bf16[2,256,512]{2,1,0:T(8,128)(2,1)S(1)}, bf16[2,256,512]{2,1,0:T(8,128)(2,1)S(1)}, u32[]{:S(2)}, u32[]{:S(2)}) collective-permute-start(bf16[2,256,512]{2,1,0:T(8,128)(2,1)S(1)} %get-tuple-element.310), channel_id=1, source_target_pairs={{0,1},{1,2},{2,3},{4,5},{5,6},{6,7},{8,9},{9,10},{10,11},{12,13},{... | collective-permute-start | bytes 1572872 | tf_op jit(solution)/shard_map/ppermute | solution.py:23
  110.8 15.2 %collective-permute-start.1 = (bf16[2,256,512]{2,1,0:T(8,128)(2,1)S(1)}, bf16[2,256,512]{2,1,0:T(8,128)(2,1)}, u32[]{:S(2)}, u32[]{:S(2)}) collective-permute-start(bf16[2,256,512]{2,1,0:T(8,128)(2,1)S(1)} %get-tuple-element.311), channel_id=1, source_target_pairs={{1,0},{2,1},{3,2},{5,4},{6,5},{7,6},{9,8},{10,9},{11,10},{13,12},{... | collective-permute-start | bytes 1572872 | tf_op jit(solution)/shard_map/ppermute | solution.py:26
  112.1 16.2 %copy-start.4 = (f32[512]{0:T(512)S(1)}, f32[512]{0:T(512)}, u32[]{:S(2)}) copy-start(f32[512]{0:T(512)} %param.13) | copy-start | bytes 6148
  112.1 16.2 %copy-start.5 = (s32[256]{0:T(256)S(1)}, s32[256]{0:T(256)}, u32[]{:S(2)}) copy-start(s32[256]{0:T(256)} %param.11) | copy-start | bytes 3076
  112.1 16.2 %copy-start.6 = (s32[256]{0:T(256)S(1)}, s32[256]{0:T(256)}, u32[]{:S(2)}) copy-start(s32[256]{0:T(256)} %param.12) | copy-start | bytes 3076
  112.1 16.2 %copy-start.7 = (s32[256]{0:T(256)S(1)}, s32[256]{0:T(256)}, u32[]{:S(2)}) copy-start(s32[256]{0:T(256)} %param.10) | copy-start | bytes 3076
  122.0 0.8 copy-start.3
  246.2 0.9 copy-start.1
